TPU v7x, 256 devices: a whole 4x4x8 slice. The times are simulated.
256 devices in a mesh: ma: 64 (over x, z, core), row: 4 (over y).
Axes of the slice: x: 4, y: 4, z: 8, core: 2. Of those that a mesh axis runs over, the one named last changes fastest.
Arguments:
- fields: bfloat16 [6, 64, 2, 512, 512], P(None, 'row', None, 'ma'), may hold values from -6 to 6
- legendre: bfloat16 [512, 512, 768], P('ma'), may hold values from -0.25 to 0.25
- quad: float32 [768], replicated, may hold values from 0.1 to 1.9
- assign: int32 [512], replicated, may hold values from 0 to 511, each once
Outputs:
- induction: float32 [3, 64, 2, 512, 512], P(None, 'row', None, 'ma')
Inputs may be any that keep to these rules, and one draw needn't show every extreme that they name: assign holds each order 0 to 511 exactly once; order slot s of fields, legendre and induction belongs to order assign[s].
All inputs are finite; a program needn't handle non-finite values.
Results may differ from a plain program's by a relative error of at most 0.0068.
Values may be sent and summed in bfloat16 or wider, within the bound.
A program may use at most 128 MiB of HBM per device.

v0:
```python
import math

import jax
import jax.numpy as jnp
from jax import lax
from jax.sharding import PartitionSpec as P

NLON = 1536


def padded_2(block, sides, width):
    for axis, dim in sides:
        count = lax.axis_size(axis)
        forward = [(i, i + 1) for i in range(count - 1)]
        backward = [(target, source) for source, target in forward]
        low = lax.ppermute(
            lax.slice_in_dim(block, block.shape[dim] - width, None, axis=dim), axis, forward
        )
        high = lax.ppermute(lax.slice_in_dim(block, 0, width, axis=dim), axis, backward)
        block = jnp.concatenate([low, block, high], axis=dim)
    return block


def longitude_tables(assign, lon_count):
    lon_index = jnp.arange(lon_count, dtype=jnp.int32)
    phase_angle = (assign[:, None] * lon_index[None, :] % lon_count).astype(jnp.float32) * (
        2.0 * math.pi / lon_count
    )
    order_total = assign.shape[0]
    factor = jnp.where(assign > 0, 2.0, 1.0).astype(jnp.float32) / math.sqrt(order_total)
    cosine = jnp.cos(phase_angle)
    sine_part = jnp.sin(phase_angle)
    synth_table = jnp.stack([factor[:, None] * cosine, -factor[:, None] * sine_part]).astype(
        jnp.bfloat16
    )
    analysis_table = (jnp.stack([cosine, -sine_part]) / math.sqrt(lon_count)).astype(jnp.bfloat16)
    return (synth_table, analysis_table)


def shards(fields, legendre, quad, assign):
    slot_count = legendre.shape[0]
    ma_index = lax.axis_index("ma")
    orders = lax.dynamic_slice_in_dim(assign, ma_index * slot_count, slot_count)
    degree = jnp.arange(legendre.shape[1], dtype=jnp.int32)
    keep_mask = (degree[None, :] >= orders[:, None]).astype(jnp.bfloat16)
    synth_table, analysis_table = longitude_tables(assign, NLON)
    levels = fields.shape[1]
    total_levels = levels * lax.axis_size("row")
    level_base = lax.axis_index("row") * levels
    masked = fields * keep_mask[None, None, None]
    latitude_data = lax.all_to_all(
        jnp.einsum("slj,fkcsl->sjfkc", legendre, masked, preferred_element_type=jnp.float32).astype(
            jnp.bfloat16
        ),
        "ma",
        split_axis=1,
        concat_axis=0,
        tiled=True,
    )
    physical = jnp.einsum(
        "sjfkc,csn->jfkn", latitude_data, synth_table, preferred_element_type=jnp.float32
    )
    vel_r, vel_t, vel_p, mag_r, mag_t, mag_p = [physical[:, index] for index in range(6)]
    emf_radial = vel_t * mag_p - vel_p * mag_t
    emf_theta = vel_p * mag_r - vel_r * mag_p
    emf_phi = vel_r * mag_t - vel_t * mag_r
    level_count = physical.shape[2]
    global_level = level_base + jnp.arange(level_count, dtype=jnp.int32)
    radius = 0.5 + (global_level.astype(jnp.float32) + 0.5) / total_levels
    scaled_emf = (radius[None, None, :, None] * jnp.stack([emf_theta, emf_phi])).astype(
        jnp.bfloat16
    )
    padded = padded_2(scaled_emf, (("row", 2),), 1)
    below_level = padded[:, :, :-2].astype(jnp.float32)
    middle = padded[:, :, 1:-1].astype(jnp.float32)
    above_level = padded[:, :, 2:].astype(jnp.float32)
    middle_level = level_base + jnp.arange(levels, dtype=jnp.int32)
    at_bottom = (middle_level == 0)[None, None, :, None]
    at_top = (middle_level == total_levels - 1)[None, None, :, None]
    centered = 0.5 * (above_level - below_level)
    radial_diff = jnp.where(
        at_bottom, above_level - middle, jnp.where(at_top, middle - below_level, centered)
    )
    middle_radius = (0.5 + (middle_level.astype(jnp.float32) + 0.5) / total_levels)[None, :, None]
    curl_theta = -radial_diff[1] / middle_radius
    curl_phi = radial_diff[0] / middle_radius
    curl_parts = jnp.stack([emf_radial, curl_theta, curl_phi], axis=1).astype(jnp.bfloat16)
    longitude_coef = jnp.einsum(
        "jgkn,csn->jgkcs", curl_parts, analysis_table, preferred_element_type=jnp.float32
    )
    lat_count = curl_parts.shape[0]
    weights = lax.dynamic_slice_in_dim(quad, ma_index * lat_count, lat_count)
    weighted = (longitude_coef * weights[:, None, None, None, None]).astype(jnp.bfloat16)
    keep_float = keep_mask.astype(jnp.float32)

    def forward(exchanged):
        values = jnp.einsum(
            "jgkcs,slj->sgkcl", exchanged, legendre, preferred_element_type=jnp.float32
        )
        values = values * keep_float[:, None, None, None, :]
        return jnp.transpose(values, (1, 2, 3, 0, 4))

    return forward(lax.all_to_all(weighted, "ma", split_axis=4, concat_axis=0, tiled=True))


def solution(mesh):
    return jax.shard_map(
        shards,
        mesh=mesh,
        in_specs=(P(None, "row", None, "ma", None), P("ma", None, None), P(), P()),
        out_specs=P(None, "row", None, "ma", None),
        check_vma=False,
    )
```

profile of v0, /device:TPU:1, one launch (start us, length us, event | category | flops | bytes accessed | tf_op | source)
XLA Modules:
  0.0 332.0 jit_solution(17358624820358124304)
XLA Ops:
  0.8 1.5 broadcast_multiply_fusion
  2.3 5.4 %convert_bitcast_fusion = bf16[8,768,6,16,2]{1,3,4,2,0:T(8,128)(2,1)S(1)} fusion(bf16[8,512,768]{2,1,0:T(8,128)(2,1)} %param.5, bf16[6,16,2,8,512]{4,3,2,1,0:T(8,128)(2,1)S(1)} %broadcast_multiply_fusion), kind=kOutput, calls=%fused_computation.38 | convolution fusion | flops 1209139200 | bytes 10223616 | tf_op jit(solution)/shard_map/slj,fkcsl->sjfkc/dot_general | solution.py:52
  7.8 33.7 %copy.35 = bf16[8,768,6,16,2]{3,4,2,0,1:T(2,128)(2,1)} copy(bf16[8,768,6,16,2]{1,3,4,2,0:T(8,128)(2,1)S(1)} %convert_bitcast_fusion) | data formatting | bytes 4718592 | tf_op jit(solution)/shard_map/convert_element_type | solution.py:52
  41.5 22.4 %reshape.333 = bf16[64,2,9216]{2,1,0:T(2,128)(2,1)} reshape(bf16[768,8,6,2,16]{4,3,2,1,0:T(2,128)(2,1)} %bitcast.116) | data formatting | bytes 4718592
  63.9 13.1 %all-to-all-start = ((bf16[64,2,9216]{2,1,0:T(2,128)(2,1)}), bf16[64,2,9216]{2,1,0:T(2,128)(2,1)S(1)}, u32[]{:S(2)}, u32[]{:S(2)}) async-start(bf16[64,2,9216]{2,1,0:T(2,128)(2,1)} %reshape.333), calls=%async_computation | async-start | bytes 4718592 | tf_op jit(solution)/shard_map/all_to_all | solution.py:51
  77.8 16.2 %multiply_convert_fusion.1 = (bf16[1,512,1536]{2,1,0:T(8,128)(2,1)}, f32[1,512,1536]{2,1,0:T(8,128)}, bf16[1,512,1536]{2,1,0:T(8,128)(2,1)}, f32[1,512,1536]{2,1,0:T(8,128)}) fusion(f32[512]{0:T(512)S(1)} %get-tuple-element.15, s32[512]{0:T(512)S(1)} %copy-done.2, f32[512]{0:T(512)S(1)} %get-tuple-element.16), kind=kLoop, calls=%fused_computation.21 | loop fusion | flops 11010048 | bytes 9443328 | tf_op jit(solution)/shard_map/convert.3
  94.0 39.6 %all-to-all-done = bf16[64,2,9216]{2,1,0:T(2,128)(2,1)S(1)} async-done(((bf16[64,2,9216]{2,1,0:T(2,128)(2,1)}), bf16[64,2,9216]{2,1,0:T(2,128)(2,1)S(1)}, u32[]{:S(2)}, u32[]{:S(2)}) %all-to-all-start) | async-done | bytes 2359328 | tf_op jit(solution)/shard_map/all_to_all | solution.py:51
  133.6 15.4 %reshape.334 = bf16[768,8,6,2,16]{4,3,2,1,0:T(2,128)(2,1)} reshape(bf16[64,2,9216]{2,1,0:T(2,128)(2,1)S(1)} %all-to-all-done) | data formatting | bytes 4718592
  149.0 14.1 %fusion.8 = f32[12,6,16,1536]{3,2,1,0:T(8,128)S(1)} fusion(bf16[8,64,12,6,16,2]{4,5,3,0,2,1:T(2,128)(2,1)} %bitcast.115, bf16[1,512,1536]{2,1,0:T(8,128)(2,1)} %get-tuple-element.13, bf16[1,512,1536]{2,1,0:T(8,128)(2,1)} %get-tuple-element.11), kind=kOutput, calls=%fused_computation.11 | convolution fusion | flops 3625451520 | bytes 12582912 | tf_op jit(solution)/shard_map/sjfkc,csn->jfkn/dot_general | solution.py:60
  164.9 3.2 collective-permute-start.1
  168.1 1.5 collective-permute-start
  169.6 1.4 collective-permute-done.1
  171.0 3.8 %collective-permute-done = bf16[2,12,1,1536]{3,2,1,0:T(2,128)(2,1)S(1)} collective-permute-done((bf16[2,12,1,1536]{3,2,1,0:T(2,128)(2,1)S(1)}, bf16[2,12,1,1536]{3,2,1,0:T(2,128)(2,1)S(1)}, u32[]{:S(2)}, u32[]{:S(2)}) %collective-permute-start) | collective-permute-done | bytes 73760 | tf_op jit(solution)/shard_map/ppermute | solution.py:19
  176.7 1.4 copy-done
  178.1 2.1 multiply_convert_fusion.2
  180.2 16.8 %copy.48 = bf16[12,3,16,2,512]{2,3,1,0,4:T(2,128)(2,1)} copy(bf16[12,3,16,2,512]{4,2,3,1,0:T(8,128)(2,1)S(1)} %multiply_convert_fusion.2) | data formatting | bytes 2359296 | tf_op jit(solution)/shard_map/convert_element_type | solution.py:93
  197.0 26.0 %reshape.335 = bf16[64,2,4608]{2,1,0:T(2,128)(2,1)S(1)} reshape(bf16[512,12,3,2,16]{4,3,2,1,0:T(2,128)(2,1)} %bitcast.117) | data formatting | bytes 2359296
  223.0 37.7 %all_to_all.36 = bf16[64,2,4608]{2,1,0:T(2,128)(2,1)S(1)} all-to-all(bf16[64,2,4608]{2,1,0:T(2,128)(2,1)S(1)} %reshape.335), channel_id=1, replica_groups=mesh['ma'=64,'row'=4] {'ma'}, dimensions={0} | all-to-all | bytes 2359296 | tf_op jit(solution)/shard_map/all_to_all | solution.py:103
  260.7 8.1 %reshape.336 = bf16[512,12,3,2,16]{4,3,2,1,0:T(2,128)(2,1)} reshape(bf16[64,2,4608]{2,1,0:T(2,128)(2,1)S(1)} %all_to_all.36) | data formatting | bytes 2359296
  268.8 9.6 %copy.83 = bf16[12,3,16,2,512]{2,4,3,1,0:T(8,128)(2,1)} copy(bf16[12,3,16,2,512]{2,3,1,0,4:T(2,128)(2,1)} %bitcast.118) | data formatting | bytes 2359296 | tf_op jit(solution)/shard_map/all_to_all | solution.py:103
  278.4 23.1 %copy.63 = bf16[64,12,3,16,2,8]{1,0,3,4,2,5:T(8,128)(2,1)} copy(bf16[64,12,3,16,2,8]{3,5,0,4,2,1:T(8,128)(2,1)} %bitcast.119) | data formatting | bytes 2359296 | tf_op jit(solution)/shard_map/all_to_all | solution.py:103
  301.5 23.6 %reshape.332 = bf16[768,3,16,2,8]{0,2,3,1,4:T(8,128)(2,1)S(1)} reshape(bf16[64,12,3,16,2,8]{1,0,3,4,2,5:T(8,128)(2,1)} %copy.63) | data formatting | bytes 2359296 | tf_op jit(solution)/shard_map/all_to_all | solution.py:103
  325.1 4.8 %multiply_bitcast_fusion = f32[3,16,2,8,512]{4,1,2,0,3:T(8,128)S(1)} fusion(bf16[768,3,16,2,8]{0,2,3,1,4:T(8,128)(2,1)S(1)} %reshape.332, bf16[8,512,768]{2,1,0:T(8,128)(2,1)} %param.5, f32[8,512]{1,0:T(8,128)S(1)} %get-tuple-element.17), kind=kOutput, calls=%fused_computation.42 | convolution fusion | flops 604372992 | bytes 9060352 | tf_op jit(solution)/shard_map/jgkcs,slj->sgkcl/dot_general | solution.py:97
  329.9 2.1 copy.52
  (17 shorter events, 5.2 us)
Async XLA Ops:
  63.9 13.9 %copy-start.2 = (s32[512]{0:T(512)S(1)}, s32[512]{0:T(512)}, u32[]{:S(2)}) copy-start(s32[512]{0:T(512)} %param.7) | copy-start | bytes 6148
  63.9 69.7 %all-to-all-start = ((bf16[64,2,9216]{2,1,0:T(2,128)(2,1)}), bf16[64,2,9216]{2,1,0:T(2,128)(2,1)S(1)}, u32[]{:S(2)}, u32[]{:S(2)}) async-start(bf16[64,2,9216]{2,1,0:T(2,128)(2,1)} %reshape.333), calls=%async_computation | async-start | bytes 4718592 | tf_op jit(solution)/shard_map/all_to_all | solution.py:51
  164.9 6.1 %collective-permute-start.1 = (bf16[2,12,1,1536]{3,2,1,0:T(2,128)(2,1)S(1)}, bf16[2,12,1,1536]{3,2,1,0:T(2,128)(2,1)S(1)}, u32[]{:S(2)}, u32[]{:S(2)}) collective-permute-start(bf16[2,12,1,1536]{3,2,1,0:T(2,128)(2,1)S(1)} %get-tuple-element.10), channel_id=1, source_target_pairs={{0,1},{1,2},{2,3},{4,5},{5,6},{6,7},{8,9},{9,10},{10,11},{12,13},{... | collective-permute-start | bytes 221192 | tf_op jit(solution)/shard_map/ppermute | solution.py:16
  168.1 6.7 %collective-permute-start = (bf16[2,12,1,1536]{3,2,1,0:T(2,128)(2,1)S(1)}, bf16[2,12,1,1536]{3,2,1,0:T(2,128)(2,1)S(1)}, u32[]{:S(2)}, u32[]{:S(2)}) collective-permute-start(bf16[2,12,1,1536]{3,2,1,0:T(2,128)(2,1)S(1)} %get-tuple-element.9), channel_id=1, source_target_pairs={{1,0},{2,1},{3,2},{5,4},{6,5},{7,6},{9,8},{10,9},{11,10},{13,12},{... | collective-permute-start | bytes 221192 | tf_op jit(solution)/shard_map/ppermute | solution.py:19
  174.9 1.9 copy-start.1
  176.1 2.1 copy-start
where the time goes:
time: 334 us; the launch traced here: 332 us
  local copies, waits for them, and re-layouts  184 us (55%)
  waiting for transfers between devices  44.8 us (13%)
  blocking collectives  37.7 us (11%)
  matrix products  26.4 us (8%)
  other arithmetic  20.8 us (6%)
  starting transfers between devices  17.8 us (5%)
    unnamed x10, local copies, waits for them, and re-layouts  73.7 us
    all_to_all x3, local copies, waits for them, and re-layouts, shards(): lax.all_to_all(weighted, 'ma', split_axis=4, concat_axis=0, tiled=True)  56.2 us
    all_to_all x1, waiting for transfers between devices, shards(): lax.all_to_all(jnp.einsum('slj,fkcsl->sjfkc', legendre, masked, preferred...  39.6 us
    all_to_all x1, blocking collectives, shards(): lax.all_to_all(weighted, 'ma', split_axis=4, concat_axis=0, tiled=True)  37.7 us
    convert_element_type x1, local copies, waits for them, and re-layouts, shards(): jnp.einsum('slj,fkcsl->sjfkc', legendre, masked, preferred_element_type=j...  33.7 us
    another operation x3, other arithmetic  17.3 us
    convert_element_type x1, local copies, waits for them, and re-layouts, shards(): (longitude_coef * weights[:, None, None, None, None]).astype(jnp.bfloat16)  16.8 us
    dot_general x1, matrix products, shards(): jnp.einsum('sjfkc,csn->jfkn', latitude_data, synth_table, preferred_eleme...  14.1 us
  transfers between devices with their start and end apart: 3, of which 3 were waited for; matrix products, arithmetic and copies ran while one was open for 5% of the time, Pallas kernels for 0%

commit v1 on v0

v1 whole, which is shorter than its diff:
```python
import functools
import math

import jax
import jax.numpy as jnp
from jax import lax
from jax.experimental import pallas as pl
from jax.experimental.pallas import tpu as pltpu
from jax.sharding import PartitionSpec as P

NLON = 1536
F32 = jnp.float32
BF16 = jnp.bfloat16


def left_lanes(rows):
    return lax.broadcasted_iota(jnp.int32, (rows, 128), 1) < 64


def inverse_kernel(orders_ref, fields_ref, leg_ref, out_ref, coef, spat):
    s = pl.program_id(0)

    @pl.when(s == 0)
    def _():
        for t in range(4):
            coef[t] = fields_ref[:, t * 128 : t * 128 + 128].astype(F32)

    x = jnp.concatenate([coef[t, pl.ds(s, 192, stride=8), :] for t in range(4)], axis=1)
    degree = lax.broadcasted_iota(jnp.int32, x.shape, 1)
    x = jnp.where(degree >= orders_ref[s], x, 0.0).astype(BF16)
    y = jnp.dot(x, leg_ref[0], preferred_element_type=F32)
    for t in range(6):
        spat[t, pl.ds(s, 192, stride=8), :] = y[:, t * 128 : t * 128 + 128]

    @pl.when(s == 7)
    def _():
        left = left_lanes(16)

        def level(k, carry):
            for jq in range(4):
                base, odd = 3 * (jq // 2), jq % 2
                for q in range(3):
                    tile = base + odd if q < 2 else base + 2
                    high = q == 1 or (q == 2 and odd)
                    for p in range(3):
                        u = spat[tile, pl.ds(pl.multiple_of(p * 256 + k * 16, 16), 16), :]
                        b = spat[tile, pl.ds(pl.multiple_of(p * 256 + 768 + k * 16, 16), 16), :]
                        if high:
                            v = jnp.where(left, pltpu.roll(u, 64, 1), b)
                        else:
                            v = jnp.where(left, u, pltpu.roll(b, 64, 1))
                        at = (q * 3 + p) * 128
                        out_ref[k * 4 + jq, :, at : at + 128] = v.astype(BF16)
            return carry

        lax.fori_loop(0, 16, level, 0)


def inverse(orders, fields, legendre):
    return pl.pallas_call(
        inverse_kernel,
        grid_spec=pltpu.PrefetchScalarGridSpec(
            num_scalar_prefetch=1,
            grid=(8,),
            in_specs=[
                pl.BlockSpec((1536, 512), lambda s, o: (0, 0)),
                pl.BlockSpec((1, 512, 768), lambda s, o: (s, 0, 0)),
            ],
            out_specs=pl.BlockSpec((64, 16, 1152), lambda s, o: (0, 0, 0)),
            scratch_shapes=[pltpu.VMEM((4, 1536, 128), F32), pltpu.VMEM((6, 1536, 128), F32)],
        ),
        out_shape=jax.ShapeDtypeStruct((64, 16, 1152), BF16),
        name="inverse",
    )(orders, fields, legendre)


def grid_kernel(radius_ref, got_ref, synth_ref, analysis_ref, quad_ref, out_ref, emf):
    radius = radius_ref[0]
    tile_rows = 256
    left = left_lanes(tile_rows)

    def synth(i, carry):
        rows = pl.ds(pl.multiple_of(i * tile_rows, tile_rows), tile_rows)
        lines = synth_ref[rows, :]
        diffs = []
        for q in range(3):
            g = jnp.dot(
                lines, got_ref[:, q * 384 : q * 384 + 384], preferred_element_type=F32
            )
            c = [g[:, p * 128 : p * 128 + 128] for p in range(3)]
            r = [pltpu.roll(v, 64, 1) for v in c]
            d = []
            for a, b in ((1, 2), (2, 0), (0, 1)):
                t = c[a] * r[b]
                d.append(t - pltpu.roll(t, 64, 1))
            diffs.append([d[0], d[1] * radius, d[2] * radius])
        for g in range(3):
            emf[rows, g * 128 : g * 128 + 128] = jnp.where(
                left, diffs[0][g], -diffs[1][g]
            ).astype(BF16)
        emf[rows, 384:512] = jnp.where(left, diffs[2][0], -diffs[2][1]).astype(BF16)
        emf[rows, 512:640] = diffs[2][2].astype(BF16)
        return carry

    lax.fori_loop(0, NLON // tile_rows, synth, 0)

    def analyse(i, carry):
        rows = pl.ds(pl.multiple_of(i * tile_rows, tile_rows), tile_rows)
        w = jnp.dot(analysis_ref[rows, :], emf[...], preferred_element_type=F32)
        w = w * quad_ref[...]
        dests = pl.ds(i * (tile_rows // 16), tile_rows // 16)
        for t in range(4):
            block = w[:, t * 128 : t * 128 + 128].reshape(tile_rows // 16, 16, 128)
            out_ref[dests, t * 16 : t * 16 + 16, :] = block.astype(BF16)
        last = w[:, 512:640].reshape(tile_rows // 16, 16, 128)
        lane = lax.broadcasted_iota(jnp.int32, (tile_rows // 16, 8, 128), 2)
        pair = jnp.where(lane < 64, last[:, :8], -last[:, 8:])
        out_ref[dests, 64:72, :] = pair.astype(BF16)
        return carry

    lax.fori_loop(0, 1024 // tile_rows, analyse, 0)


def grid_space(radius, got, synth, analysis, quad_lanes):
    vmem = pl.BlockSpec(memory_space=pltpu.VMEM)
    return pl.pallas_call(
        grid_kernel,
        in_specs=[pl.BlockSpec(memory_space=pltpu.SMEM), vmem, vmem, vmem, vmem],
        out_specs=vmem,
        scratch_shapes=[pltpu.VMEM((NLON, 640), BF16)],
        out_shape=jax.ShapeDtypeStruct((64, 72, 128), BF16),
        name="grid",
    )(radius, got, synth, analysis, quad_lanes)


def forward_kernel(orders_ref, got_ref, low_ref, high_ref, coef_ref, leg_ref, out_ref, full, lhs, done):
    s = pl.program_id(0)

    @pl.when(s == 0)
    def _():
        left = left_lanes(16)
        left8 = left_lanes(8)

        def unpack(block, first, level):
            base = pl.multiple_of(level * 16, 16)
            for pair in range(2):
                ev, od = first + pair * 2, first + pair * 2 + 1
                lanes = [pair * 3 + t for t in range(3)]
                for g in (1, 2):
                    rows = pl.ds(pl.multiple_of((g - 1) * 288 + base, 16), 16)
                    full[lanes[0], rows, :] = block(ev, g * 16, 16)
                    full[lanes[1], rows, :] = block(od, g * 16, 16)
                e, o = block(ev, 48, 16), block(od, 48, 16)
                full[lanes[2], pl.ds(base, 16), :] = jnp.where(
                    left, pltpu.roll(e, 64, 1), o
                )
                e, o = block(ev, 64, 8), block(od, 64, 8)
                full[lanes[2], pl.ds(pl.multiple_of(288 + base, 16), 8), :] = jnp.where(
                    left8, e, pltpu.roll(o, 64, 1)
                )
                full[lanes[2], pl.ds(pl.multiple_of(296 + base, 8), 8), :] = jnp.where(
                    left8, pltpu.roll(e, 64, 1), o
                )

        unpack(lambda i, at, n: low_ref[i, at : at + n, :].astype(F32), 0, 0)
        unpack(lambda i, at, n: high_ref[i, at : at + n, :].astype(F32), 0, 17)

        def level(k, carry):
            block = lambda i, at, n: got_ref[i, at : at + n, :].astype(F32)
            unpack(block, k * 4, k + 1)
            for pair in range(2):
                ev, od = k * 4 + pair * 2, k * 4 + pair * 2 + 1
                rows = pl.ds(pl.multiple_of(k * 16, 16), 16)
                lhs[pair * 3, rows, :] = block(ev, 0, 16)
                lhs[pair * 3 + 1, rows, :] = block(od, 0, 16)
                lhs[pair * 3 + 2, rows, :] = jnp.where(
                    left, block(ev, 48, 16), pltpu.roll(block(od, 48, 16), 64, 1)
                )
            return carry

        lax.fori_loop(0, 16, level, 0)

        def derive(k, carry):
            up, mid, down = coef_ref[0, k], coef_ref[1, k], coef_ref[2, k]

            def diff(at):
                here = lambda n: full[:, pl.ds(pl.multiple_of(at + (k + n) * 16, 16), 16), :]
                return up * here(2) + mid * here(1) + down * here(0)

            lhs[:, pl.ds(pl.multiple_of(256 + k * 16, 16), 16), :] = -diff(288)
            lhs[:, pl.ds(pl.multiple_of(512 + k * 16, 16), 16), :] = diff(0)
            return carry

        lax.fori_loop(0, 16, derive, 0)

    x = jnp.concatenate([lhs[t, pl.ds(s, 96, stride=8), :] for t in range(6)], axis=1)
    x = x.astype(BF16)
    y = lax.dot_general(x, leg_ref[0], (((1,), (1,)), ((), ())), preferred_element_type=F32)
    degree = lax.broadcasted_iota(jnp.int32, y.shape, 1)
    y = jnp.where(degree >= orders_ref[s], y, 0.0)
    for t in range(4):
        done[t, pl.ds(s, 96, stride=8), :] = y[:, t * 128 : t * 128 + 128]

    @pl.when(s == 7)
    def _():
        for t in range(4):
            out_ref[:, t * 128 : t * 128 + 128] = done[t]


def forward(orders, got, low, high, coef, legendre):
    fixed = lambda *shape: pl.BlockSpec(shape, lambda s, o: (0,) * len(shape))
    return pl.pallas_call(
        forward_kernel,
        grid_spec=pltpu.PrefetchScalarGridSpec(
            num_scalar_prefetch=1,
            grid=(8,),
            in_specs=[
                fixed(64, 72, 128),
                fixed(4, 72, 128),
                fixed(4, 72, 128),
                pl.BlockSpec(memory_space=pltpu.SMEM),
                pl.BlockSpec((1, 512, 768), lambda s, o: (s, 0, 0)),
            ],
            out_specs=fixed(768, 512),
            scratch_shapes=[pltpu.VMEM((6, 576, 128), F32), pltpu.VMEM((6, 768, 128), F32), pltpu.VMEM((4, 768, 128), F32)],
        ),
        out_shape=jax.ShapeDtypeStruct((768, 512), F32),
        name="forward",
    )(orders, got, low, high, coef, legendre)


def tables(assign):
    order = jnp.tile(assign.reshape(64, 1, 8), (1, 2, 1)).reshape(1024)
    shift = jnp.tile(jnp.array([0, NLON // 4], jnp.int32)[None, :, None], (64, 1, 8)).reshape(1024)
    lon = jnp.arange(NLON, dtype=jnp.int32)
    factor = jnp.where(order > 0, 2.0, 1.0).astype(F32) / math.sqrt(assign.shape[0])
    step = 2.0 * math.pi / NLON
    down = jnp.cos(((lon[:, None] * order[None, :] + shift[None, :]) % NLON).astype(F32) * step)
    synth = (factor[None, :] * down).astype(BF16)
    across = jnp.cos(((order[:, None] * lon[None, :] + shift[:, None]) % NLON).astype(F32) * step)
    analysis = (across / math.sqrt(NLON)).astype(BF16)
    return synth, analysis


def shards(fields, legendre, quad, assign):
    ma = lax.axis_index("ma")
    row = lax.axis_index("row")
    rows = lax.axis_size("row")
    levels = fields.shape[1]
    total = levels * rows
    orders = lax.dynamic_slice_in_dim(assign, ma * 8, 8)

    packed = inverse(orders, fields.reshape(1536, 512), legendre)
    got = lax.all_to_all(packed, "ma", split_axis=0, concat_axis=0, tiled=True)

    synth, analysis = tables(assign)
    level = row * levels + ma // 4
    radius = 0.5 + (level.astype(F32) + 0.5) / total
    jq = ma % 4
    first = (3 * (jq // 2) + jq % 2) * 128
    second = (3 * (jq // 2) + 2) * 128 + (jq % 2) * 64
    pair = lax.dynamic_slice_in_dim(quad, first, 128)
    half = lax.dynamic_slice_in_dim(quad, second, 64)
    quad_lanes = jnp.concatenate([pair, pair, pair, half, half, half, half])[None, :]

    out = grid_space(radius[None], got.reshape(1024, 1152), synth, analysis, quad_lanes)
    back = lax.all_to_all(out, "ma", split_axis=0, concat_axis=0, tiled=True)

    up = [(i, i + 1) for i in range(rows - 1)]
    down = [(b, a) for a, b in up]
    low = lax.ppermute(back[60:], "row", up)
    high = lax.ppermute(back[:4], "row", down)

    index = row * levels + jnp.arange(levels, dtype=jnp.int32)
    inv = 1.0 / (0.5 + (index.astype(F32) + 0.5) / total)
    bottom, top = index == 0, index == total - 1
    coef = jnp.stack(
        [
            jnp.where(top, 0.0, jnp.where(bottom, 1.0, 0.5)) * inv,
            jnp.where(bottom, -1.0, jnp.where(top, 1.0, 0.0)) * inv,
            jnp.where(bottom, 0.0, jnp.where(top, -1.0, -0.5)) * inv,
        ]
    )
    result = forward(orders, back, low, high, coef, legendre)
    return result.reshape(3, levels, 2, 8, 512)


def solution(mesh):
    return jax.shard_map(
        shards,
        mesh=mesh,
        in_specs=(P(None, "row", None, "ma", None), P("ma", None, None), P(), P()),
        out_specs=P(None, "row", None, "ma", None),
        check_vma=False,
    )
```

time: 334 us -> 160 us (0.48)
  local copies, waits for them, and re-layouts: 184 us -> 6.12 us
  blocking collectives: 37.7 us -> 0 us
  Pallas kernels: 0 us -> 37.3 us
  other arithmetic: 20.8 us -> 53 us
  matrix products: 26.4 us -> 0 us
  starting transfers between devices: 17.8 us -> 26.2 us
  waiting for transfers between devices: 44.8 us -> 36.5 us
    unnamed x10, local copies, waits for them, and re-layouts: 73.7 us -> 2.13 us
    all_to_all x3 -> x0, local copies, waits for them, and re-layouts: 56.2 us -> none  [shards(): lax.all_to_all(weighted, 'ma', split_axis=4, concat_axis=0, tiled=True)]
    convert_element_type x2, other arithmetic: 0.37 us -> 52.3 us  [the longest x1 26.7 us: tables(): analysis = (across / math.sqrt(NLON)).astype(BF16)]
    convert_element_type x2 -> x0, local copies, waits for them, and re-layouts: 50.5 us -> none  [the longest x1 33.7 us: shards(): jnp.einsum('slj,fkcsl->sjfkc', legendre, masked, preferred_element_type=j...]
    all_to_all x1 -> x0, blocking collectives: 37.7 us -> none  [shards(): lax.all_to_all(weighted, 'ma', split_axis=4, concat_axis=0, tiled=True)]
    pallas_call x0 -> x3, Pallas kernels: none -> 37.3 us  [the longest x1 14.7 us: grid_space(): pl.pallas_call(grid_kernel, in_specs=[pl.BlockSpec(memory_space=pltpu.SME...]
    dot_general x4 -> x0, matrix products: 26.4 us -> none  [the longest x1 14.1 us: shards(): jnp.einsum('sjfkc,csn->jfkn', latitude_data, synth_table, preferred_eleme...]
    another operation x3 -> x2, other arithmetic: 17.3 us -> 0.61 us  [the longest x1 0.6 us: shards(): jnp.stack([jnp.where(top, 0.0, jnp.where(bottom, 1.0, 0.5)) * inv, jnp.wh...]
  transfers between devices with their start and end apart: 3 -> 4, of which waited for: 3 -> 3; matrix products, arithmetic and copies ran while one was open for 5% -> 35% of each run, Pallas kernels for 0% -> 0%
where the time goes in v1:
time: 160 us; the launch traced here: 159 us
  other arithmetic  53 us (33%)
  Pallas kernels  37.3 us (23%)
  waiting for transfers between devices  36.5 us (23%)
  starting transfers between devices  26.2 us (16%)
  local copies, waits for them, and re-layouts  6.12 us (4%)
    all_to_all x1, waiting for transfers between devices, shards(): back = lax.all_to_all(out, 'ma', split_axis=0, concat_axis=0, tiled=True)  31.3 us
    convert_element_type x1, other arithmetic, tables(): analysis = (across / math.sqrt(NLON)).astype(BF16)  26.7 us
    convert_element_type x1, other arithmetic, tables(): synth = (factor[None, :] * down).astype(BF16)  25.6 us
    pallas_call x1, Pallas kernels, grid_space(): pl.pallas_call(grid_kernel, in_specs=[pl.BlockSpec(memory_space=pltpu.SME...  14.7 us
    all_to_all x1, starting transfers between devices, shards(): got = lax.all_to_all(packed, 'ma', split_axis=0, concat_axis=0, tiled=True)  13 us
    pallas_call x1, Pallas kernels, inverse(): pl.pallas_call(inverse_kernel, grid_spec=pltpu.PrefetchScalarGridSpec(num...  11.7 us
    pallas_call x1, Pallas kernels, forward(): pl.pallas_call(forward_kernel, grid_spec=pltpu.PrefetchScalarGridSpec(num...  10.9 us
    all_to_all x1, starting transfers between devices, shards(): back = lax.all_to_all(out, 'ma', split_axis=0, concat_axis=0, tiled=True)  8.77 us
  transfers between devices with their start and end apart: 4, of which 3 were waited for; matrix products, arithmetic and copies ran while one was open for 35% of the time, Pallas kernels for 0%

profile of v1, /device:TPU:1, one launch (start us, length us, event | category | flops | bytes accessed | tf_op | source)
XLA Modules:
  0.0 159.3 jit_solution(150838849094643269)
XLA Ops:
  0.0 1.3 dynamic_slice.9.orders_ref
  1.3 11.7 %inverse.1 = bf16[64,16,1152]{2,1,0:T(8,128)(2,1)} custom-call(s32[8]{0:T(128)} %dynamic_slice.9.orders_ref, bf16[1536,512]{1,0:T(8,128)(2,1)} %bitcast.9, bf16[8,512,768]{2,1,0:T(8,128)(2,1)} %leg_ref.3), custom_call_target="tpu_custom_call" | custom-call | tf_op jit(solution)/shard_map/inverse/pallas_call | solution.py:60
  13.0 13.0 %all-to-all-start = ((bf16[64,16,1152]{2,1,0:T(8,128)(2,1)}), bf16[64,16,1152]{2,1,0:T(8,128)(2,1)S(1)}, u32[]{:S(2)}, u32[]{:S(2)}) async-start(bf16[64,16,1152]{2,1,0:T(8,128)(2,1)} %inverse.1), calls=%async_computation | async-start | bytes 4718592 | tf_op jit(solution)/shard_map/all_to_all | solution.py:254
  26.1 0.1 tile.16
  26.1 0.8 dynamic_slice.11
  26.9 0.8 dynamic_slice.10
  27.7 0.1 concatenate.3
  27.8 0.6 broadcast_in_dim.42.quad_ref
  28.4 0.1 tile.18
  28.5 0.1 tile.19
  28.6 0.1 tile.20
  28.7 25.6 %fusion.4.synth_ref = bf16[1536,1024]{1,0:T(8,128)(2,1)} fusion(s32[1024]{0:T(1024)S(1)} %tile.20, s32[1024]{0:T(1024)S(1)} %tile.18, f32[1024]{0:T(1024)S(1)} %select_multiply_fusion), kind=kLoop, calls=%fused_computation.6 | loop fusion | flops 18874368 | bytes 3158016 | tf_op jit(solution)/shard_map/convert_element_type | solution.py:239
  54.3 26.7 %fusion.9.analysis_ref = bf16[1024,1536]{1,0:T(8,128)(2,1)} fusion(s32[1024]{0:T(1024)S(1)} %tile.20, s32[1024]{0:T(1024)S(1)} %tile.18), kind=kLoop, calls=%fused_computation.11 | loop fusion | flops 18874368 | bytes 3153920 | tf_op jit(solution)/shard_map/convert_element_type | solution.py:241
  81.0 1.6 all-to-all-done
  82.6 1.5 copy-done
  84.1 14.7 %grid.1 = bf16[64,72,128]{2,1,0:T(8,128)(2,1)} custom-call(f32[1]{0:T(128)} %bitcast.radius_ref, bf16[1024,1152]{1,0:T(8,128)(2,1)} %bitcast.8, bf16[1536,1024]{1,0:T(8,128)(2,1)} %fusion.4.synth_ref, bf16[1024,1536]{1,0:T(8,128)(2,1)} %fusion.9.analysis_ref, f32[1,640]{1,0:T(1,128)} %broadcast_in_dim.42.quad_ref), custom_call_target="tpu_custom_call" | custom-call | tf_op jit(solution)/shard_map/grid/pallas_call | solution.py:126
  98.8 8.8 %all-to-all-start.1 = ((bf16[64,72,128]{2,1,0:T(8,128)(2,1)}), bf16[64,72,128]{2,1,0:T(8,128)(2,1)S(1)}, u32[]{:S(2)}, u32[]{:S(2)}) async-start(bf16[64,72,128]{2,1,0:T(8,128)(2,1)} %grid.1), calls=%async_computation.1 | async-start | bytes 2359296 | tf_op jit(solution)/shard_map/all_to_all | solution.py:267
  107.6 31.3 %all-to-all-done.1.got_ref = bf16[64,72,128]{2,1,0:T(8,128)(2,1)S(1)} async-done(((bf16[64,72,128]{2,1,0:T(8,128)(2,1)}), bf16[64,72,128]{2,1,0:T(8,128)(2,1)S(1)}, u32[]{:S(2)}, u32[]{:S(2)}) %all-to-all-start.1) | async-done | bytes 1179680 | tf_op jit(solution)/shard_map/all_to_all | solution.py:267
  138.9 3.2 %collective-permute-start = (bf16[4,72,128]{2,1,0:T(8,128)(2,1)S(1)}, bf16[4,72,128]{2,1,0:T(8,128)(2,1)S(1)}, u32[]{:S(2)}, u32[]{:S(2)}) collective-permute-start(bf16[4,72,128]{2,1,0:T(8,128)(2,1)S(1)} %get-tuple-element.6), channel_id=1, source_target_pairs={{0,1},{1,2},{2,3},{4,5},{5,6},{6,7},{8,9},{9,10},{10,11},{12,13},{... | collective-permute-start | bytes 221192 | tf_op jit(solution)/shard_map/ppermute | solution.py:271
  142.1 1.3 collective-permute-start.1
  143.4 0.6 pad_maximum_fusion.coef_ref
  144.1 3.7 %collective-permute-done.1.high_ref = bf16[4,72,128]{2,1,0:T(8,128)(2,1)S(1)} collective-permute-done((bf16[4,72,128]{2,1,0:T(8,128)(2,1)S(1)}, bf16[4,72,128]{2,1,0:T(8,128)(2,1)S(1)}, u32[]{:S(2)}, u32[]{:S(2)}) %collective-permute-start.1) | collective-permute-done | bytes 73760 | tf_op jit(solution)/shard_map/ppermute | solution.py:272
  147.7 0.6 copy-done.3
  148.4 10.9 %forward.1 = f32[768,512]{1,0:T(8,128)} custom-call(s32[8]{0:T(128)} %dynamic_slice.9.orders_ref, bf16[64,72,128]{2,1,0:T(8,128)(2,1)} %copy-done.1, bf16[4,72,128]{2,1,0:T(8,128)(2,1)} %copy-done.2, bf16[4,72,128]{2,1,0:T(8,128)(2,1)} %copy-done.3, f32[3,16]{1,0:T(4,128)} %pad_maximum_fusion.coef_ref, bf16[8,512,768]{2,1,0:T(8,128)(2,1)} %leg_ref.3), custom_call_target="tpu_custom_call" | custom-call | tf_op jit(solution)/shard_map/forward/pallas_call | solution.py:212
  (15 shorter events, 0.1 us)
Async XLA Ops:
  1.3 24.7 %copy-start.4 = (s32[512]{0:T(512)S(1)}, s32[512]{0:T(512)}, u32[]{:S(2)}) copy-start(s32[512]{0:T(512)} %param.8) | copy-start | bytes 6148
  13.0 69.6 %all-to-all-start = ((bf16[64,16,1152]{2,1,0:T(8,128)(2,1)}), bf16[64,16,1152]{2,1,0:T(8,128)(2,1)S(1)}, u32[]{:S(2)}, u32[]{:S(2)}) async-start(bf16[64,16,1152]{2,1,0:T(8,128)(2,1)} %inverse.1), calls=%async_computation | async-start | bytes 4718592 | tf_op jit(solution)/shard_map/all_to_all | solution.py:254
  82.6 1.5 copy-start
  98.8 40.1 %all-to-all-start.1 = ((bf16[64,72,128]{2,1,0:T(8,128)(2,1)}), bf16[64,72,128]{2,1,0:T(8,128)(2,1)S(1)}, u32[]{:S(2)}, u32[]{:S(2)}) async-start(bf16[64,72,128]{2,1,0:T(8,128)(2,1)} %grid.1), calls=%async_computation.1 | async-start | bytes 2359296 | tf_op jit(solution)/shard_map/all_to_all | solution.py:267
  138.9 8.8 %copy-start.1 = (bf16[64,72,128]{2,1,0:T(8,128)(2,1)}, bf16[64,72,128]{2,1,0:T(8,128)(2,1)S(1)}, u32[]{:S(2)}) copy-start(bf16[64,72,128]{2,1,0:T(8,128)(2,1)S(1)} %all-to-all-done.1.got_ref) | copy-start | bytes 3538948
  138.9 5.1 %collective-permute-start = (bf16[4,72,128]{2,1,0:T(8,128)(2,1)S(1)}, bf16[4,72,128]{2,1,0:T(8,128)(2,1)S(1)}, u32[]{:S(2)}, u32[]{:S(2)}) collective-permute-start(bf16[4,72,128]{2,1,0:T(8,128)(2,1)S(1)} %get-tuple-element.6), channel_id=1, source_target_pairs={{0,1},{1,2},{2,3},{4,5},{5,6},{6,7},{8,9},{9,10},{10,11},{12,13},{... | collective-permute-start | bytes 221192 | tf_op jit(solution)/shard_map/ppermute | solution.py:271
  142.1 5.6 %collective-permute-start.1 = (bf16[4,72,128]{2,1,0:T(8,128)(2,1)S(1)}, bf16[4,72,128]{2,1,0:T(8,128)(2,1)S(1)}, u32[]{:S(2)}, u32[]{:S(2)}) collective-permute-start(bf16[4,72,128]{2,1,0:T(8,128)(2,1)S(1)} %get-tuple-element.5), channel_id=1, source_target_pairs={{1,0},{2,1},{3,2},{5,4},{6,5},{7,6},{9,8},{10,9},{11,10},{13,12},{... | collective-permute-start | bytes 221192 | tf_op jit(solution)/shard_map/ppermute | solution.py:272
  144.1 3.7 %copy-start.2 = (bf16[4,72,128]{2,1,0:T(8,128)(2,1)}, bf16[4,72,128]{2,1,0:T(8,128)(2,1)S(1)}, u32[]{:S(2)}) copy-start(bf16[4,72,128]{2,1,0:T(8,128)(2,1)S(1)} %collective-permute-done.low_ref) | copy-start | bytes 221188
  147.7 0.6 copy-start.3

commit v2 on v0

v2 whole, which is shorter than its diff:
```python
import math

import jax
import jax.numpy as jnp
import numpy as np
from jax import lax
from jax.experimental import pallas as pl
from jax.experimental.pallas import tpu as pltpu
from jax.sharding import PartitionSpec as P

NLON = 1536
PEERS = 64
F32 = jnp.float32
BF16 = jnp.bfloat16
MESH = pl.DeviceIdType.MESH


def fit(function, terms):
    z = 0.125 - 0.1251 * np.cos(np.pi * (np.arange(400) + 0.5) / 400)
    z = np.clip(z, 1e-12, None)
    values = function(np.sqrt(z))
    basis = np.polynomial.Chebyshev.fit(z, values, terms - 1, domain=[0.0, 0.25])
    power = basis.convert(kind=np.polynomial.Polynomial)
    return [float(c) for c in power.coef]


COS = fit(lambda t: np.cos(2 * np.pi * t), 9)
SIN = fit(lambda t: np.sin(2 * np.pi * t) / t, 9)


def horner(coefs, z):
    total = jnp.full(z.shape, coefs[-1], F32)
    for c in coefs[-2::-1]:
        total = total * z + c
    return total


def cos_sin(product):
    turns = jnp.floor(product * (1.0 / NLON) + 0.5)
    t = (product - turns * NLON) * (1.0 / NLON)
    z = t * t
    return horner(COS, z), t * horner(SIN, z)


def aligned(value, size):
    return pl.ds(pl.multiple_of(value, size), size)


def kernel(
    assign_ref, lanes_ref, quad_ref, fields_hbm, leg_hbm, out_ref,
    fbuf, coef, xs, leg, spat, send1, recv1, synth, analysis, cb, sb, ca, sa,
    emf, send2, recv2, low, high, full, lhs, done,
    in_sem, ssem1, rsem1, lsem1, ssem2, rsem2, lsem2, hsend, hrecv,
):
    me = lax.axis_index("ma")
    row = lax.axis_index("row")
    rows = lax.axis_size("row")
    above = lax.rem(row + 1, rows)
    below = lax.rem(row + rows - 1, rows)
    total = 16 * rows

    fetch = pltpu.make_async_copy(fields_hbm, fbuf, in_sem.at[8])
    fetch.start()
    fetches = [pltpu.make_async_copy(leg_hbm.at[s], leg.at[s], in_sem.at[s]) for s in range(8)]
    for f in fetches:
        f.start()

    barrier = pltpu.get_barrier_semaphore()

    def greet(i, carry):
        pl.semaphore_signal(
            barrier, inc=1, device_id={"ma": lax.rem(me + i, PEERS)}, device_id_type=MESH
        )
        return carry

    lax.fori_loop(1, PEERS, greet, 0)
    for other in (above, below):
        pl.semaphore_signal(barrier, inc=1, device_id={"row": other}, device_id_type=MESH)

    left = lax.broadcasted_iota(jnp.int32, (16, 128), 1) < 64

    fetch.wait()
    for t in range(4):
        coef[t] = fbuf[:, t * 128 : t * 128 + 128].astype(F32)

    def mask(s, carry):
        order = assign_ref[me * 8 + s]
        for t in range(4):
            x = coef[t, pl.ds(s, 192, stride=8), :]
            degree = lax.broadcasted_iota(jnp.int32, x.shape, 1) + t * 128
            xs[s, :, t * 128 : t * 128 + 128] = jnp.where(degree >= order, x, 0.0).astype(BF16)
        return carry

    lax.fori_loop(0, 8, mask, 0)

    def level_group(i):
        half = (i + 1) // 2
        odd = lax.rem(i, 2)
        return lax.rem(me // 4 + odd * half + (1 - odd) * (16 - half), 16)

    def issue1(q, i):
        k = level_group(i)
        for jq in range(4):
            dest = k * 4 + jq

            @pl.when(dest != me)
            def _():
                pltpu.make_async_remote_copy(
                    src_ref=send1.at[q, dest],
                    dst_ref=recv1.at[q, me],
                    send_sem=ssem1.at[q],
                    recv_sem=rsem1.at[q],
                    device_id={"ma": dest},
                    device_id_type=MESH,
                ).start()

            @pl.when(dest == me)
            def _():
                pltpu.make_async_copy(send1.at[q, dest], recv1.at[q, me], lsem1.at[q]).start()

    for q in range(3):
        for s in range(8):
            if q == 0:
                fetches[s].wait()
            table = jnp.concatenate(
                [leg[s, :, q * 128 : q * 128 + 128], leg[s, :, q * 128 + 384 : q * 128 + 512]],
                axis=1,
            )
            y = jnp.dot(xs[s], table, preferred_element_type=F32)
            spat[0, pl.ds(s, 192, stride=8), :] = y[:, :128]
            spat[1, pl.ds(s, 192, stride=8), :] = y[:, 128:]

        if q == 0:
            pl.semaphore_wait(barrier, PEERS + 1)

        def group(i, carry):
            k = level_group(i)
            for jq in range(4):
                for p in range(3):
                    u = spat[jq // 2, aligned(p * 256 + k * 16, 16), :]
                    b = spat[jq // 2, aligned(p * 256 + 768 + k * 16, 16), :]
                    if jq % 2:
                        v = jnp.where(left, pltpu.roll(u, 64, 1), b)
                    else:
                        v = jnp.where(left, u, pltpu.roll(b, 64, 1))
                    send1[q, k * 4 + jq, :, p * 128 : p * 128 + 128] = v.astype(BF16)

            @pl.when(i > 0)
            def _():
                issue1(q, i - 1)

            return carry

        lax.fori_loop(0, 16, group, 0)
        issue1(q, 15)

    m = lanes_ref[...].astype(F32)
    lane = lax.broadcasted_iota(jnp.int32, (16, 1024), 1)
    second = lax.rem(lane // 8, 2) == 1
    n1 = lax.broadcasted_iota(jnp.int32, (16, 1024), 0).astype(F32) * 128.0
    c, s_ = cos_sin(n1 * m)
    ca[...] = jnp.where(second, -s_, c)
    sa[...] = jnp.where(second, c, s_)

    def fine(i, carry):
        n0 = (lax.broadcasted_iota(jnp.int32, (16, 1024), 0) + i * 16).astype(F32)
        c, s_ = cos_sin(n0 * m)
        cb[aligned(i * 16, 16), :] = c
        sb[aligned(i * 16, 16), :] = s_
        return carry

    lax.fori_loop(0, 8, fine, 0)
    factor = jnp.where(m > 0.0, 2.0, 1.0) * (1.0 / math.sqrt(PEERS * 8))
    for n in range(NLON // 128):
        cn = ca[n : n + 1, :] * factor
        sn = sa[n : n + 1, :] * factor

        def fill(i, carry):
            at = aligned(i * 16, 16)
            synth[aligned(n * 128 + i * 16, 16), :] = (cn * cb[at, :] - sn * sb[at, :]).astype(BF16)
            return carry

        lax.fori_loop(0, 8, fill, 0)

    def across(i, carry):
        at = aligned(i * 128, 128)
        cbt, sbt = cb[:, at].T, sb[:, at].T
        cat, sat = ca[:, at].T, sa[:, at].T
        scale = 1.0 / math.sqrt(NLON)
        cat, sat = cat * scale, sat * scale
        for n in range(NLON // 128):
            v = cat[:, n : n + 1] * cbt - sat[:, n : n + 1] * sbt
            analysis[at, n * 128 : n * 128 + 128] = v.astype(BF16)
        return carry

    lax.fori_loop(0, 8, across, 0)

    jq = lax.rem(me, 4)
    level = row * 16 + me // 4
    radius = 0.5 + (level.astype(F32) + 0.5) * (1.0 / total)
    lane1 = lax.broadcasted_iota(jnp.int32, (1, 128), 1)
    mine = lane1 // 64 == lax.rem(jq, 2)
    left_tall = lax.broadcasted_iota(jnp.int32, (256, 128), 1) < 64

    def issue2(q, i):
        tile = lax.rem(me // 16 + i, 4)

        def one(j, carry):
            dest = tile * 16 + lax.rem(me + j, 16)

            @pl.when(dest != me)
            def _():
                pltpu.make_async_remote_copy(
                    src_ref=send2.at[q, dest],
                    dst_ref=recv2.at[q, me],
                    send_sem=ssem2.at[q],
                    recv_sem=rsem2.at[q],
                    device_id={"ma": dest},
                    device_id_type=MESH,
                ).start()

            @pl.when(dest == me)
            def _():
                pltpu.make_async_copy(send2.at[q, dest], recv2.at[q, me], lsem2.at[q]).start()

            return carry

        lax.fori_loop(0, 16, one, 0)

    for q in range(3):
        span = recv1.at[q, pl.ds(0, PEERS - 1)]
        pltpu.make_async_copy(span, span, rsem1.at[q]).wait()
        pltpu.make_async_copy(recv1.at[q, 0], recv1.at[q, 0], lsem1.at[q]).wait()
        quads = quad_ref[pl.ds((jq // 2) * 3 + q, 1), :]
        quads = jnp.where(mine, quads, pltpu.roll(quads, 64, 1))

        def synthesise(i, carry):
            at = aligned(i * 256, 256)
            got = recv1[q].reshape(1024, 384)
            g = jnp.dot(synth[at, :], got, preferred_element_type=F32)
            c = [g[:, p * 128 : p * 128 + 128] for p in range(3)]
            r = [pltpu.roll(v, 64, 1) for v in c]
            d = []
            for a, b in ((1, 2), (2, 0), (0, 1)):
                t = c[a] * r[b]
                d.append(t - pltpu.roll(t, 64, 1))
            emf[at, 0:128] = jnp.where(left_tall, d[0], -(d[1] * radius)).astype(BF16)
            emf[at, 128:256] = (d[2] * radius).astype(BF16)
            return carry

        lax.fori_loop(0, NLON // 256, synthesise, 0)

        def analyse(i, carry):
            tile = lax.rem(me // 16 + i, 4)
            w = jnp.dot(analysis[aligned(tile * 256, 256), :], emf[...], preferred_element_type=F32)
            dests = aligned(tile * 16, 16)
            send2[q, dests, 0:16, :] = (w[:, :128] * quads).reshape(16, 16, 128).astype(BF16)
            last = (w[:, 128:] * quads).reshape(16, 16, 128)
            lane3 = lax.broadcasted_iota(jnp.int32, (16, 8, 128), 2)
            pair = jnp.where(lane3 < 64, last[:, :8], -last[:, 8:])
            send2[q, dests, 16:24, :] = pair.astype(BF16)

            @pl.when(i > 0)
            def _():
                issue2(q, i - 1)

            return carry

        lax.fori_loop(0, 4, analyse, 0)
        issue2(q, 3)

    left8 = lax.broadcasted_iota(jnp.int32, (8, 128), 1) < 64

    def halos(q):
        up = pltpu.make_async_remote_copy(
            src_ref=recv2.at[q, pl.ds(60, 4)],
            dst_ref=low.at[q],
            send_sem=hsend.at[2 * q],
            recv_sem=hrecv.at[2 * q],
            device_id={"row": above},
            device_id_type=MESH,
        )
        down = pltpu.make_async_remote_copy(
            src_ref=recv2.at[q, pl.ds(0, 4)],
            dst_ref=high.at[q],
            send_sem=hsend.at[2 * q + 1],
            recv_sem=hrecv.at[2 * q + 1],
            device_id={"row": below},
            device_id_type=MESH,
        )
        return up, down

    def unpack(block, first, slot, k):
        base = slot * 16
        for pair in range(2):
            ev, od = first + pair * 2, first + pair * 2 + 1
            e, o = block(ev, 0, 16), block(od, 0, 16)
            if k is not None:
                lhs[pair, aligned(k * 16, 16), :] = jnp.where(left, e, pltpu.roll(o, 64, 1))
            full[pair, aligned(base, 16), :] = jnp.where(left, pltpu.roll(e, 64, 1), o)
            e, o = block(ev, 16, 8), block(od, 16, 8)
            full[pair, aligned(288 + base, 8), :] = jnp.where(left8, e, pltpu.roll(o, 64, 1))
            full[pair, aligned(296 + base, 8), :] = jnp.where(left8, pltpu.roll(e, 64, 1), o)

    for q in range(3):
        span = recv2.at[q, pl.ds(0, PEERS - 1)]
        pltpu.make_async_copy(span, span, rsem2.at[q]).wait()
        pltpu.make_async_copy(recv2.at[q, 0], recv2.at[q, 0], lsem2.at[q]).wait()
        up, down = halos(q)
        up.start()
        down.start()

        def own(k, carry):
            unpack(lambda i, at, n: recv2[q, i, at : at + n, :].astype(F32), k * 4, k + 1, k)
            return carry

        lax.fori_loop(0, 16, own, 0)
        up.wait_recv()
        down.wait_recv()
        unpack(lambda i, at, n: low[q, i, at : at + n, :].astype(F32), 0, 0, None)
        unpack(lambda i, at, n: high[q, i, at : at + n, :].astype(F32), 0, 17, None)

        def derive(k, carry):
            index = row * 16 + k
            r = 0.5 + (jnp.full((16, 128), index.astype(F32), F32) + 0.5) * (1.0 / total)
            inv = 1.0 / r
            bottom, top = index == 0, index == total - 1
            hi = jnp.where(top, 0.0, jnp.where(bottom, 1.0, 0.5)) * inv
            mid = jnp.where(bottom, -1.0, jnp.where(top, 1.0, 0.0)) * inv
            lo = jnp.where(bottom, 0.0, jnp.where(top, -1.0, -0.5)) * inv
            for pair in range(2):

                def diff(at):
                    here = lambda n: full[pair, aligned(at + (k + n) * 16, 16), :]
                    return hi * here(2) + mid * here(1) + lo * here(0)

                lhs[pair, aligned(256 + k * 16, 16), :] = -diff(288)
                lhs[pair, aligned(512 + k * 16, 16), :] = diff(0)
            return carry

        lax.fori_loop(0, 16, derive, 0)

        for s in range(8):
            x = jnp.concatenate(
                [lhs[0, pl.ds(s, 96, stride=8), :], lhs[1, pl.ds(s, 96, stride=8), :]], axis=1
            ).astype(BF16)
            table = jnp.concatenate(
                [leg[s, :, q * 128 : q * 128 + 128], leg[s, :, q * 128 + 384 : q * 128 + 512]],
                axis=1,
            )
            y = lax.dot_general(x, table, (((1,), (1,)), ((), ())), preferred_element_type=F32)
            if q == 2:
                degree = lax.broadcasted_iota(jnp.int32, y.shape, 1)
                y = jnp.where(degree >= assign_ref[me * 8 + s], done[s] + y, 0.0)
                for t in range(4):
                    coef[t, pl.ds(s, 96, stride=8), :] = y[:, t * 128 : t * 128 + 128]
            else:
                done[s] = y if q == 0 else done[s] + y

    for t in range(4):
        out_ref[:, t * 128 : t * 128 + 128] = coef[t, 0:768, :]

    for q in range(3):
        span = send1.at[q, pl.ds(0, PEERS - 1)]
        pltpu.make_async_copy(span, span, ssem1.at[q]).wait()
        span = send2.at[q, pl.ds(0, PEERS - 1)]
        pltpu.make_async_copy(span, span, ssem2.at[q]).wait()
        up, down = halos(q)
        up.wait_send()
        down.wait_send()


def shards(fields, legendre, quad, assign):
    order = jnp.broadcast_to(assign.reshape(64, 1, 8), (64, 2, 8)).reshape(1, 1024)
    vmem = pl.BlockSpec(memory_space=pltpu.VMEM)
    hbm = pl.BlockSpec(memory_space=pl.ANY)
    dma = pltpu.SemaphoreType.DMA
    result = pl.pallas_call(
        kernel,
        in_specs=[pl.BlockSpec(memory_space=pltpu.SMEM), vmem, vmem, hbm, hbm],
        out_specs=vmem,
        out_shape=jax.ShapeDtypeStruct((768, 512), F32),
        scratch_shapes=[
            pltpu.VMEM((1536, 512), BF16),
            pltpu.VMEM((4, 1536, 128), F32),
            pltpu.VMEM((8, 192, 512), BF16),
            pltpu.VMEM((8, 512, 768), BF16),
            pltpu.VMEM((2, 1536, 128), F32),
            pltpu.VMEM((3, PEERS, 16, 384), BF16),
            pltpu.VMEM((3, PEERS, 16, 384), BF16),
            pltpu.VMEM((NLON, 1024), BF16),
            pltpu.VMEM((1024, NLON), BF16),
            pltpu.VMEM((128, 1024), F32),
            pltpu.VMEM((128, 1024), F32),
            pltpu.VMEM((16, 1024), F32),
            pltpu.VMEM((16, 1024), F32),
            pltpu.VMEM((NLON, 256), BF16),
            pltpu.VMEM((3, PEERS, 24, 128), BF16),
            pltpu.VMEM((3, PEERS, 24, 128), BF16),
            pltpu.VMEM((3, 4, 24, 128), BF16),
            pltpu.VMEM((3, 4, 24, 128), BF16),
            pltpu.VMEM((2, 576, 128), F32),
            pltpu.VMEM((2, 768, 128), F32),
            pltpu.VMEM((8, 96, 512), F32),
            dma((9,)),
            dma((3,)),
            dma((3,)),
            dma((3,)),
            dma((3,)),
            dma((3,)),
            dma((3,)),
            dma((6,)),
            dma((6,)),
        ],
        compiler_params=pltpu.CompilerParams(collective_id=0, has_side_effects=True),
        name="induction",
    )(assign, order, quad.reshape(6, 128), fields.reshape(1536, 512), legendre)
    return result.reshape(3, 16, 2, 8, 512)


def solution(mesh):
    return jax.shard_map(
        shards,
        mesh=mesh,
        in_specs=(P(None, "row", None, "ma", None), P("ma", None, None), P(), P()),
        out_specs=P(None, "row", None, "ma", None),
        check_vma=False,
    )
```

time: 334 us -> 102 us (0.31)
  local copies, waits for them, and re-layouts: 184 us -> 4.29 us
  Pallas kernels: 0 us -> 97.5 us
  waiting for transfers between devices: 44.8 us -> 0 us
  blocking collectives: 37.7 us -> 0 us
  matrix products: 26.4 us -> 0 us
  other arithmetic: 20.8 us -> 0 us
  starting transfers between devices: 17.8 us -> 0 us
    pallas_call x0 -> x1, Pallas kernels: none -> 97.5 us  [shards(): pl.pallas_call(kernel, in_specs=[pl.BlockSpec(memory_space=pltpu.SMEM), v...]
    unnamed x10 -> x1, local copies, waits for them, and re-layouts: 73.7 us -> 2.77 us
    all_to_all x3 -> x0, local copies, waits for them, and re-layouts: 56.2 us -> none  [shards(): lax.all_to_all(weighted, 'ma', split_axis=4, concat_axis=0, tiled=True)]
    convert_element_type x2 -> x0, local copies, waits for them, and re-layouts: 50.5 us -> none  [the longest x1 33.7 us: shards(): jnp.einsum('slj,fkcsl->sjfkc', legendre, masked, preferred_element_type=j...]
    all_to_all x1 -> x0, waiting for transfers between devices: 39.6 us -> none  [shards(): lax.all_to_all(jnp.einsum('slj,fkcsl->sjfkc', legendre, masked, preferred...]
    all_to_all x1 -> x0, blocking collectives: 37.7 us -> none  [shards(): lax.all_to_all(weighted, 'ma', split_axis=4, concat_axis=0, tiled=True)]
    dot_general x4 -> x0, matrix products: 26.4 us -> none  [the longest x1 14.1 us: shards(): jnp.einsum('sjfkc,csn->jfkn', latitude_data, synth_table, preferred_eleme...]
    another operation x3 -> x0, other arithmetic: 17.3 us -> none
  transfers between devices with their start and end apart: 3 -> 0, of which waited for: 3 -> 0; matrix products, arithmetic and copies ran while one was open for 5% -> 0% of each run, Pallas kernels for 0% -> 0%
where the time goes in v2:
time: 102 us
  Pallas kernels  97.5 us (96%)
  local copies, waits for them, and re-layouts  4.29 us (4%)
    pallas_call x1, Pallas kernels, shards(): pl.pallas_call(kernel, in_specs=[pl.BlockSpec(memory_space=pltpu.SMEM), v...  97.5 us
    unnamed x1, local copies, waits for them, and re-layouts  2.77 us

profile of v2, /device:TPU:1, one launch (start us, length us, event | category | flops | bytes accessed | tf_op | source)
XLA Modules:
  0.0 101.8 jit_solution(1148395500589577694)
XLA Ops:
  0.0 0.8 broadcast_in_dim.7
  0.8 0.7 reshape.14.lanes_ref
  1.5 97.5 %induction.1 = f32[768,512]{1,0:T(8,128)} custom-call(s32[512]{0:T(512)} %assign_ref.1, s32[1,1024]{1,0:T(1,128)} %reshape.14.lanes_ref, f32[6,128]{1,0:T(8,128)} %bitcast.5, bf16[1536,512]{1,0:T(8,128)(2,1)} %bitcast.4, bf16[8,512,768]{2,1,0:T(8,128)(2,1)} %leg_hbm.1), custom_call_target="tpu_custom_call" | custom-call | tf_op jit(solution)/shard_map/induction/pallas_call | solution.py:378
  99.0 2.8 %copy.6 = f32[3,16,2,8,512]{4,3,2,1,0:T(8,128)} copy(f32[3,16,2,8,512]{4,3,2,1,0:T(8,128)} %bitcast.3) | data formatting | bytes 3145728
  (1 shorter events, 0.0 us)

commit v3 on v2

--- a/solution.py
+++ b/solution.py
@@ -47,10 +47,10 @@
 
 
 def kernel(
-    assign_ref, lanes_ref, quad_ref, fields_hbm, leg_hbm, out_ref,
+    small_ref, fields_hbm, leg_hbm, out_hbm,
     fbuf, coef, xs, leg, spat, send1, recv1, synth, analysis, cb, sb, ca, sa,
-    emf, send2, recv2, low, high, full, lhs, done,
-    in_sem, ssem1, rsem1, lsem1, ssem2, rsem2, lsem2, hsend, hrecv,
+    emf, send2, recv2, send3, recv3, low, high, full, lhs, done, orders, quads,
+    in_sem, ssem1, rsem1, lsem1, ssem2, rsem2, ssem3, rsem3, hsend, hrecv,
 ):
     me = lax.axis_index("ma")
     row = lax.axis_index("row")
@@ -84,10 +84,10 @@
         coef[t] = fbuf[:, t * 128 : t * 128 + 128].astype(F32)
 
     def mask(s, carry):
-        order = assign_ref[me * 8 + s]
+        order = small_ref[me * 8 + s]
         for t in range(4):
             x = coef[t, pl.ds(s, 192, stride=8), :]
-            degree = lax.broadcasted_iota(jnp.int32, x.shape, 1) + t * 128
+            degree = (lax.broadcasted_iota(jnp.int32, x.shape, 1) + t * 128).astype(F32)
             xs[s, :, t * 128 : t * 128 + 128] = jnp.where(degree >= order, x, 0.0).astype(BF16)
         return carry
 
@@ -130,9 +130,6 @@
             spat[0, pl.ds(s, 192, stride=8), :] = y[:, :128]
             spat[1, pl.ds(s, 192, stride=8), :] = y[:, 128:]
 
-        if q == 0:
-            pl.semaphore_wait(barrier, PEERS + 1)
-
         def group(i, carry):
             k = level_group(i)
             for jq in range(4):
@@ -145,16 +142,44 @@
                         v = jnp.where(left, u, pltpu.roll(b, 64, 1))
                     send1[q, k * 4 + jq, :, p * 128 : p * 128 + 128] = v.astype(BF16)
 
-            @pl.when(i > 0)
-            def _():
-                issue1(q, i - 1)
+            if q > 0:
+
+                @pl.when(i > 0)
+                def _():
+                    issue1(q, i - 1)
 
             return carry
 
         lax.fori_loop(0, 16, group, 0)
+        if q == 0:
+            pl.semaphore_wait(barrier, PEERS + 1)
+
+            def send(i, carry):
+                issue1(0, i)
+                return carry
+
+            lax.fori_loop(0, 15, send, 0)
         issue1(q, 15)
 
-    m = lanes_ref[...].astype(F32)
+    lane1 = lax.broadcasted_iota(jnp.int32, (1, 128), 1)
+    slot = (lane1 // 16) * 8 + lax.rem(lane1, 8)
+
+    def spread(i, carry):
+        held = jnp.zeros((1, 128), F32)
+        for n in range(64):
+            held = jnp.where(slot == n, small_ref[i * 64 + n], held)
+        orders[0:1, aligned(i * 128, 128)] = held
+        return carry
+
+    lax.fori_loop(0, 8, spread, 0)
+    jq = lax.rem(me, 4)
+    for q in range(3):
+        first = ((jq // 2) * 3 + q) * 128 + lax.rem(jq, 2) * 64
+        held = jnp.zeros((1, 128), F32)
+        for n in range(64):
+            held = jnp.where(lax.rem(lane1, 64) == n, small_ref[PEERS * 8 + first + n], held)
+        quads[q : q + 1, :] = held
+    m = orders[0:1, :]
     lane = lax.broadcasted_iota(jnp.int32, (16, 1024), 1)
     second = lax.rem(lane // 8, 2) == 1
     n1 = lax.broadcasted_iota(jnp.int32, (16, 1024), 0).astype(F32) * 128.0
@@ -195,14 +220,11 @@
 
     lax.fori_loop(0, 8, across, 0)
 
-    jq = lax.rem(me, 4)
     level = row * 16 + me // 4
     radius = 0.5 + (level.astype(F32) + 0.5) * (1.0 / total)
-    lane1 = lax.broadcasted_iota(jnp.int32, (1, 128), 1)
-    mine = lane1 // 64 == lax.rem(jq, 2)
     left_tall = lax.broadcasted_iota(jnp.int32, (256, 128), 1) < 64
 
-    def issue2(q, i):
+    def issue2(q, i, source, target, ssem, rsem):
         tile = lax.rem(me // 16 + i, 4)
 
         def one(j, carry):
@@ -211,28 +233,33 @@
             @pl.when(dest != me)
             def _():
                 pltpu.make_async_remote_copy(
-                    src_ref=send2.at[q, dest],
-                    dst_ref=recv2.at[q, me],
-                    send_sem=ssem2.at[q],
-                    recv_sem=rsem2.at[q],
+                    src_ref=source.at[q, dest],
+                    dst_ref=target.at[q, me],
+                    send_sem=ssem.at[q],
+                    recv_sem=rsem,
                     device_id={"ma": dest},
                     device_id_type=MESH,
                 ).start()
 
             @pl.when(dest == me)
             def _():
-                pltpu.make_async_copy(send2.at[q, dest], recv2.at[q, me], lsem2.at[q]).start()
+                pltpu.make_async_copy(source.at[q, dest], target.at[q, me], rsem).start()
 
             return carry
 
         lax.fori_loop(0, 16, one, 0)
+
+    def issue_parts(q, i):
+        issue2(q, i, send2, recv2, ssem2, rsem2.at[q, me // 4])
+
+    def issue_radial(q, i):
+        issue2(q, i, send3, recv3, ssem3, rsem3.at[q])
 
     for q in range(3):
         span = recv1.at[q, pl.ds(0, PEERS - 1)]
         pltpu.make_async_copy(span, span, rsem1.at[q]).wait()
         pltpu.make_async_copy(recv1.at[q, 0], recv1.at[q, 0], lsem1.at[q]).wait()
-        quads = quad_ref[pl.ds((jq // 2) * 3 + q, 1), :]
-        quads = jnp.where(mine, quads, pltpu.roll(quads, 64, 1))
+        weight = quads[q : q + 1, :]
 
         def synthesise(i, carry):
             at = aligned(i * 256, 256)
@@ -244,8 +271,8 @@
             for a, b in ((1, 2), (2, 0), (0, 1)):
                 t = c[a] * r[b]
                 d.append(t - pltpu.roll(t, 64, 1))
-            emf[at, 0:128] = jnp.where(left_tall, d[0], -(d[1] * radius)).astype(BF16)
-            emf[at, 128:256] = (d[2] * radius).astype(BF16)
+            emf[at, 0:128] = (jnp.where(left_tall, d[1], -d[2]) * radius).astype(BF16)
+            emf[at, 128:256] = d[0].astype(BF16)
             return carry
 
         lax.fori_loop(0, NLON // 256, synthesise, 0)
@@ -254,20 +281,22 @@
             tile = lax.rem(me // 16 + i, 4)
             w = jnp.dot(analysis[aligned(tile * 256, 256), :], emf[...], preferred_element_type=F32)
             dests = aligned(tile * 16, 16)
-            send2[q, dests, 0:16, :] = (w[:, :128] * quads).reshape(16, 16, 128).astype(BF16)
-            last = (w[:, 128:] * quads).reshape(16, 16, 128)
+            send2[q, dests] = (w[:, :128] * weight).reshape(16, 16, 128).astype(BF16)
+            last = (w[:, 128:] * weight).reshape(16, 16, 128)
             lane3 = lax.broadcasted_iota(jnp.int32, (16, 8, 128), 2)
             pair = jnp.where(lane3 < 64, last[:, :8], -last[:, 8:])
-            send2[q, dests, 16:24, :] = pair.astype(BF16)
+            send3[q, dests] = pair.astype(BF16)
 
             @pl.when(i > 0)
             def _():
-                issue2(q, i - 1)
+                issue_parts(q, i - 1)
 
             return carry
 
         lax.fori_loop(0, 4, analyse, 0)
-        issue2(q, 3)
+        issue_parts(q, 3)
+        for i in range(4):
+            issue_radial(q, i)
 
     left8 = lax.broadcasted_iota(jnp.int32, (8, 128), 1) < 64
 
@@ -290,35 +319,39 @@
         )
         return up, down
 
-    def unpack(block, first, slot, k):
-        base = slot * 16
+    def unpack(block, first, level):
         for pair in range(2):
-            ev, od = first + pair * 2, first + pair * 2 + 1
-            e, o = block(ev, 0, 16), block(od, 0, 16)
-            if k is not None:
-                lhs[pair, aligned(k * 16, 16), :] = jnp.where(left, e, pltpu.roll(o, 64, 1))
-            full[pair, aligned(base, 16), :] = jnp.where(left, pltpu.roll(e, 64, 1), o)
-            e, o = block(ev, 16, 8), block(od, 16, 8)
-            full[pair, aligned(288 + base, 8), :] = jnp.where(left8, e, pltpu.roll(o, 64, 1))
-            full[pair, aligned(296 + base, 8), :] = jnp.where(left8, pltpu.roll(e, 64, 1), o)
+            e, o = block(first + pair * 2), block(first + pair * 2 + 1)
+            full[pair, aligned(level * 16, 16), :] = jnp.where(left, e, pltpu.roll(o, 64, 1))
+            full[pair, aligned(288 + level * 16, 16), :] = jnp.where(left, pltpu.roll(e, 64, 1), o)
+
+    puts = [
+        pltpu.make_async_copy(
+            coef.at[t, pl.ds(0, 768)], out_hbm.at[:, pl.ds(t * 128, 128)], in_sem.at[t]
+        )
+        for t in range(4)
+    ]
 
     for q in range(3):
-        span = recv2.at[q, pl.ds(0, PEERS - 1)]
-        pltpu.make_async_copy(span, span, rsem2.at[q]).wait()
-        pltpu.make_async_copy(recv2.at[q, 0], recv2.at[q, 0], lsem2.at[q]).wait()
         up, down = halos(q)
-        up.start()
-        down.start()
-
-        def own(k, carry):
-            unpack(lambda i, at, n: recv2[q, i, at : at + n, :].astype(F32), k * 4, k + 1, k)
+
+        def own(n, carry):
+            k = lax.rem(me // 16 + 4 - n // 4, 4) * 4 + lax.rem(n, 4)
+            span = recv2.at[q, pl.ds(k * 4, 4)]
+            pltpu.make_async_copy(span, span, rsem2.at[q, k]).wait()
+
+            @pl.when(k == 15)
+            def _():
+                up.start()
+
+            @pl.when(k == 0)
+            def _():
+                down.start()
+
+            unpack(lambda i: recv2[q, i].astype(F32), k * 4, k + 1)
             return carry
 
         lax.fori_loop(0, 16, own, 0)
-        up.wait_recv()
-        down.wait_recv()
-        unpack(lambda i, at, n: low[q, i, at : at + n, :].astype(F32), 0, 0, None)
-        unpack(lambda i, at, n: high[q, i, at : at + n, :].astype(F32), 0, 17, None)
 
         def derive(k, carry):
             index = row * 16 + k
@@ -338,47 +371,78 @@
                 lhs[pair, aligned(512 + k * 16, 16), :] = diff(0)
             return carry
 
-        lax.fori_loop(0, 16, derive, 0)
-
-        for s in range(8):
-            x = jnp.concatenate(
-                [lhs[0, pl.ds(s, 96, stride=8), :], lhs[1, pl.ds(s, 96, stride=8), :]], axis=1
-            ).astype(BF16)
-            table = jnp.concatenate(
-                [leg[s, :, q * 128 : q * 128 + 128], leg[s, :, q * 128 + 384 : q * 128 + 512]],
-                axis=1,
-            )
-            y = lax.dot_general(x, table, (((1,), (1,)), ((), ())), preferred_element_type=F32)
+        lax.fori_loop(1, 15, derive, 0)
+        up.wait_recv()
+        down.wait_recv()
+        unpack(lambda i: low[q, i].astype(F32), 0, 0)
+        unpack(lambda i: high[q, i].astype(F32), 0, 17)
+        derive(0, 0)
+        derive(15, 0)
+
+        pltpu.make_async_copy(recv3.at[q], recv3.at[q], rsem3.at[q]).wait()
+
+        def radial(k, carry):
+            for pair in range(2):
+                e = recv3[q, k * 4 + pair * 2].astype(F32)
+                o = recv3[q, k * 4 + pair * 2 + 1].astype(F32)
+                lhs[pair, aligned(k * 16, 8), :] = jnp.where(left8, e, pltpu.roll(o, 64, 1))
+                lhs[pair, aligned(k * 16 + 8, 8), :] = jnp.where(left8, pltpu.roll(e, 64, 1), o)
+            return carry
+
+        lax.fori_loop(0, 16, radial, 0)
+
+        for half in range(2):
+            lines = slice(half * 256, half * 256 + 256)
+            for s in range(8):
+                x = jnp.concatenate(
+                    [lhs[0, pl.ds(s, 96, stride=8), :], lhs[1, pl.ds(s, 96, stride=8), :]], axis=1
+                ).astype(BF16)
+                table = jnp.concatenate(
+                    [
+                        leg[s, lines, q * 128 : q * 128 + 128],
+                        leg[s, lines, q * 128 + 384 : q * 128 + 512],
+                    ],
+                    axis=1,
+                )
+                y = lax.dot_general(x, table, (((1,), (1,)), ((), ())), preferred_element_type=F32)
+                if q > 0:
+                    y = done[s, :, lines] + y
+                if q < 2:
+                    done[s, :, lines] = y
+                else:
+                    degree = lax.broadcasted_iota(jnp.int32, y.shape, 1) + half * 256
+                    y = jnp.where(degree.astype(F32) >= small_ref[me * 8 + s], y, 0.0)
+                    for t in range(2):
+                        coef[half * 2 + t, pl.ds(s, 96, stride=8), :] = y[:, t * 128 : t * 128 + 128]
             if q == 2:
-                degree = lax.broadcasted_iota(jnp.int32, y.shape, 1)
-                y = jnp.where(degree >= assign_ref[me * 8 + s], done[s] + y, 0.0)
-                for t in range(4):
-                    coef[t, pl.ds(s, 96, stride=8), :] = y[:, t * 128 : t * 128 + 128]
-            else:
-                done[s] = y if q == 0 else done[s] + y
-
-    for t in range(4):
-        out_ref[:, t * 128 : t * 128 + 128] = coef[t, 0:768, :]
+                for t in range(half * 2, half * 2 + 2):
+                    puts[t].start()
 
     for q in range(3):
         span = send1.at[q, pl.ds(0, PEERS - 1)]
         pltpu.make_async_copy(span, span, ssem1.at[q]).wait()
         span = send2.at[q, pl.ds(0, PEERS - 1)]
         pltpu.make_async_copy(span, span, ssem2.at[q]).wait()
+        span = send3.at[q, pl.ds(0, PEERS - 1)]
+        pltpu.make_async_copy(span, span, ssem3.at[q]).wait()
         up, down = halos(q)
         up.wait_send()
         down.wait_send()
+    for put in puts:
+        put.wait()
 
 
 def shards(fields, legendre, quad, assign):
-    order = jnp.broadcast_to(assign.reshape(64, 1, 8), (64, 2, 8)).reshape(1, 1024)
-    vmem = pl.BlockSpec(memory_space=pltpu.VMEM)
-    hbm = pl.BlockSpec(memory_space=pl.ANY)
+    small = lax.pad(assign, jnp.int32(0), [(0, quad.shape[0], 0)]).astype(F32) + lax.pad(
+        quad, F32(0), [(assign.shape[0], 0, 0)]
+    )
+    smem = pl.BlockSpec(memory_space=pltpu.SMEM)
+    hbm = pl.BlockSpec(memory_space=pltpu.HBM)
     dma = pltpu.SemaphoreType.DMA
     result = pl.pallas_call(
         kernel,
-        in_specs=[pl.BlockSpec(memory_space=pltpu.SMEM), vmem, vmem, hbm, hbm],
-        out_specs=vmem,
+        in_specs=[smem, hbm, hbm],
+        out_specs=pl.BlockSpec(memory_space=pl.ANY),
         out_shape=jax.ShapeDtypeStruct((768, 512), F32),
         scratch_shapes=[
             pltpu.VMEM((1536, 512), BF16),
@@ -395,26 +459,33 @@
             pltpu.VMEM((16, 1024), F32),
             pltpu.VMEM((16, 1024), F32),
             pltpu.VMEM((NLON, 256), BF16),
-            pltpu.VMEM((3, PEERS, 24, 128), BF16),
-            pltpu.VMEM((3, PEERS, 24, 128), BF16),
-            pltpu.VMEM((3, 4, 24, 128), BF16),
-            pltpu.VMEM((3, 4, 24, 128), BF16),
+            pltpu.VMEM((3, PEERS, 16, 128), BF16),
+            pltpu.VMEM((3, PEERS, 16, 128), BF16),
+            pltpu.VMEM((3, PEERS, 8, 128), BF16),
+            pltpu.VMEM((3, PEERS, 8, 128), BF16),
+            pltpu.VMEM((3, 4, 16, 128), BF16),
+            pltpu.VMEM((3, 4, 16, 128), BF16),
             pltpu.VMEM((2, 576, 128), F32),
             pltpu.VMEM((2, 768, 128), F32),
             pltpu.VMEM((8, 96, 512), F32),
+            pltpu.VMEM((8, 1024), F32),
+            pltpu.VMEM((8, 128), F32),
             dma((9,)),
             dma((3,)),
             dma((3,)),
             dma((3,)),
             dma((3,)),
+            dma((3, 16)),
             dma((3,)),
             dma((3,)),
             dma((6,)),
             dma((6,)),
         ],
-        compiler_params=pltpu.CompilerParams(collective_id=0, has_side_effects=True),
+        compiler_params=pltpu.CompilerParams(
+            collective_id=0, has_side_effects=True, vmem_limit_bytes=54_000_000
+        ),
         name="induction",
-    )(assign, order, quad.reshape(6, 128), fields.reshape(1536, 512), legendre)
+    )(small, fields.reshape(1536, 512), legendre)
     return result.reshape(3, 16, 2, 8, 512)
 
 

time: 102 us -> 98.7 us (0.968)
  local copies, waits for them, and re-layouts: 4.29 us -> 1.15 us
    unnamed x1, local copies, waits for them, and re-layouts: 2.77 us -> 1.15 us
where the time goes in v3:
time: 98.7 us; the launch traced here: 98.4 us
  Pallas kernels  96.5 us (98%)
  local copies, waits for them, and re-layouts  1.15 us (1%)
    pallas_call x1, Pallas kernels, shards(): pl.pallas_call(kernel, in_specs=[smem, hbm, hbm], out_specs=pl.BlockSpec(...  96.5 us

profile of v3, /device:TPU:1, one launch (start us, length us, event | category | flops | bytes accessed | tf_op | source)
XLA Modules:
  0.0 98.4 jit_solution(2917003263528178486)
XLA Ops:
  0.0 0.7 pad_add_fusion.small_ref
  0.7 96.5 %induction.1 = f32[768,512]{1,0:T(8,128)S(1)} custom-call(f32[1280]{0:T(1024)S(1)} %pad_add_fusion.small_ref, bf16[1536,512]{1,0:T(8,128)(2,1)} %bitcast.3, bf16[8,512,768]{2,1,0:T(8,128)(2,1)} %leg_hbm.1), custom_call_target="tpu_custom_call" | custom-call | tf_op jit(solution)/shard_map/induction/pallas_call | solution.py:442
  97.2 1.1 %copy.6 = f32[3,16,2,8,512]{4,3,2,1,0:T(8,128)} copy(f32[3,16,2,8,512]{4,3,2,1,0:T(8,128)S(1)} %bitcast.2) | data formatting | bytes 3145728

commit v4 on v3

--- a/solution.py
+++ b/solution.py
@@ -49,7 +49,7 @@
 def kernel(
     small_ref, fields_hbm, leg_hbm, out_hbm,
     fbuf, coef, xs, leg, spat, send1, recv1, synth, analysis, cb, sb, ca, sa,
-    emf, send2, recv2, send3, recv3, low, high, full, lhs, done, orders, quads,
+    emf, send2, recv2, low, high, full, lhs, done, orders, quads,
     in_sem, ssem1, rsem1, lsem1, ssem2, rsem2, ssem3, rsem3, hsend, hrecv,
 ):
     me = lax.axis_index("ma")
@@ -142,24 +142,23 @@
                         v = jnp.where(left, u, pltpu.roll(b, 64, 1))
                     send1[q, k * 4 + jq, :, p * 128 : p * 128 + 128] = v.astype(BF16)
 
-            if q > 0:
-
-                @pl.when(i > 0)
-                def _():
-                    issue1(q, i - 1)
-
-            return carry
-
-        lax.fori_loop(0, 16, group, 0)
+            return carry
+
+        def group_and_send(i, carry):
+            group(i, carry)
+            issue1(q, i - lag)
+            return carry
+
+        def send(i, carry):
+            issue1(q, i)
+            return carry
+
+        lag = 3 if q == 0 else 1
+        lax.fori_loop(0, lag, group, 0)
         if q == 0:
             pl.semaphore_wait(barrier, PEERS + 1)
-
-            def send(i, carry):
-                issue1(0, i)
-                return carry
-
-            lax.fori_loop(0, 15, send, 0)
-        issue1(q, 15)
+        lax.fori_loop(lag, 16, group_and_send, 0)
+        lax.fori_loop(16 - lag, 16, send, 0)
 
     lane1 = lax.broadcasted_iota(jnp.int32, (1, 128), 1)
     slot = (lane1 // 16) * 8 + lax.rem(lane1, 8)
@@ -224,18 +223,26 @@
     radius = 0.5 + (level.astype(F32) + 0.5) * (1.0 / total)
     left_tall = lax.broadcasted_iota(jnp.int32, (256, 128), 1) < 64
 
-    def issue2(q, i, source, target, ssem, rsem):
+    def part(ref, q, index, which):
+        if q < 2:
+            return ref.at[q, index]
+        return ref.at[q, index, pl.ds(0, 16) if which == 0 else pl.ds(16, 8)]
+
+    def issue2(q, i, which):
         tile = lax.rem(me // 16 + i, 4)
+        ssem = ssem2.at[q] if which == 0 else ssem3.at[0]
+        rsem = rsem2.at[q, me // 4] if which == 0 else rsem3.at[0]
 
         def one(j, carry):
             dest = tile * 16 + lax.rem(me + j, 16)
+            source, target = part(send2, q, dest, which), part(recv2, q, me, which)
 
             @pl.when(dest != me)
             def _():
                 pltpu.make_async_remote_copy(
-                    src_ref=source.at[q, dest],
-                    dst_ref=target.at[q, me],
-                    send_sem=ssem.at[q],
+                    src_ref=source,
+                    dst_ref=target,
+                    send_sem=ssem,
                     recv_sem=rsem,
                     device_id={"ma": dest},
                     device_id_type=MESH,
@@ -243,17 +250,11 @@
 
             @pl.when(dest == me)
             def _():
-                pltpu.make_async_copy(source.at[q, dest], target.at[q, me], rsem).start()
+                pltpu.make_async_copy(source, target, rsem).start()
 
             return carry
 
         lax.fori_loop(0, 16, one, 0)
-
-    def issue_parts(q, i):
-        issue2(q, i, send2, recv2, ssem2, rsem2.at[q, me // 4])
-
-    def issue_radial(q, i):
-        issue2(q, i, send3, recv3, ssem3, rsem3.at[q])
 
     for q in range(3):
         span = recv1.at[q, pl.ds(0, PEERS - 1)]
@@ -281,28 +282,29 @@
             tile = lax.rem(me // 16 + i, 4)
             w = jnp.dot(analysis[aligned(tile * 256, 256), :], emf[...], preferred_element_type=F32)
             dests = aligned(tile * 16, 16)
-            send2[q, dests] = (w[:, :128] * weight).reshape(16, 16, 128).astype(BF16)
+            send2[q, dests, 0:16, :] = (w[:, :128] * weight).reshape(16, 16, 128).astype(BF16)
             last = (w[:, 128:] * weight).reshape(16, 16, 128)
             lane3 = lax.broadcasted_iota(jnp.int32, (16, 8, 128), 2)
             pair = jnp.where(lane3 < 64, last[:, :8], -last[:, 8:])
-            send3[q, dests] = pair.astype(BF16)
+            send2[q, dests, 16:24, :] = pair.astype(BF16)
 
             @pl.when(i > 0)
             def _():
-                issue_parts(q, i - 1)
+                issue2(q, i - 1, 0)
 
             return carry
 
         lax.fori_loop(0, 4, analyse, 0)
-        issue_parts(q, 3)
-        for i in range(4):
-            issue_radial(q, i)
+        issue2(q, 3, 0)
+        if q == 2:
+            for i in range(4):
+                issue2(q, i, 1)
 
     left8 = lax.broadcasted_iota(jnp.int32, (8, 128), 1) < 64
 
     def halos(q):
         up = pltpu.make_async_remote_copy(
-            src_ref=recv2.at[q, pl.ds(60, 4)],
+            src_ref=recv2.at[q, pl.ds(60, 4), pl.ds(0, 16)],
             dst_ref=low.at[q],
             send_sem=hsend.at[2 * q],
             recv_sem=hrecv.at[2 * q],
@@ -310,7 +312,7 @@
             device_id_type=MESH,
         )
         down = pltpu.make_async_remote_copy(
-            src_ref=recv2.at[q, pl.ds(0, 4)],
+            src_ref=recv2.at[q, pl.ds(0, 4), pl.ds(0, 16)],
             dst_ref=high.at[q],
             send_sem=hsend.at[2 * q + 1],
             recv_sem=hrecv.at[2 * q + 1],
@@ -337,7 +339,7 @@
 
         def own(n, carry):
             k = lax.rem(me // 16 + 4 - n // 4, 4) * 4 + lax.rem(n, 4)
-            span = recv2.at[q, pl.ds(k * 4, 4)]
+            span = part(recv2, q, pl.ds(k * 4, 4), 0)
             pltpu.make_async_copy(span, span, rsem2.at[q, k]).wait()
 
             @pl.when(k == 15)
@@ -348,7 +350,7 @@
             def _():
                 down.start()
 
-            unpack(lambda i: recv2[q, i].astype(F32), k * 4, k + 1)
+            unpack(lambda i: recv2[q, i, 0:16, :].astype(F32), k * 4, k + 1)
             return carry
 
         lax.fori_loop(0, 16, own, 0)
@@ -379,12 +381,14 @@
         derive(0, 0)
         derive(15, 0)
 
-        pltpu.make_async_copy(recv3.at[q], recv3.at[q], rsem3.at[q]).wait()
+        if q == 2:
+            span = part(recv2, q, pl.ds(0, PEERS), 1)
+            pltpu.make_async_copy(span, span, rsem3.at[0]).wait()
 
         def radial(k, carry):
             for pair in range(2):
-                e = recv3[q, k * 4 + pair * 2].astype(F32)
-                o = recv3[q, k * 4 + pair * 2 + 1].astype(F32)
+                e = recv2[q, k * 4 + pair * 2, 16:24, :].astype(F32)
+                o = recv2[q, k * 4 + pair * 2 + 1, 16:24, :].astype(F32)
                 lhs[pair, aligned(k * 16, 8), :] = jnp.where(left8, e, pltpu.roll(o, 64, 1))
                 lhs[pair, aligned(k * 16 + 8, 8), :] = jnp.where(left8, pltpu.roll(e, 64, 1), o)
             return carry
@@ -421,10 +425,11 @@
     for q in range(3):
         span = send1.at[q, pl.ds(0, PEERS - 1)]
         pltpu.make_async_copy(span, span, ssem1.at[q]).wait()
-        span = send2.at[q, pl.ds(0, PEERS - 1)]
+        span = part(send2, q, pl.ds(0, PEERS - 1), 0)
         pltpu.make_async_copy(span, span, ssem2.at[q]).wait()
-        span = send3.at[q, pl.ds(0, PEERS - 1)]
-        pltpu.make_async_copy(span, span, ssem3.at[q]).wait()
+        if q == 2:
+            span = part(send2, q, pl.ds(0, PEERS - 1), 1)
+            pltpu.make_async_copy(span, span, ssem3.at[0]).wait()
         up, down = halos(q)
         up.wait_send()
         down.wait_send()
@@ -459,10 +464,8 @@
             pltpu.VMEM((16, 1024), F32),
             pltpu.VMEM((16, 1024), F32),
             pltpu.VMEM((NLON, 256), BF16),
-            pltpu.VMEM((3, PEERS, 16, 128), BF16),
-            pltpu.VMEM((3, PEERS, 16, 128), BF16),
-            pltpu.VMEM((3, PEERS, 8, 128), BF16),
-            pltpu.VMEM((3, PEERS, 8, 128), BF16),
+            pltpu.VMEM((3, PEERS, 24, 128), BF16),
+            pltpu.VMEM((3, PEERS, 24, 128), BF16),
             pltpu.VMEM((3, 4, 16, 128), BF16),
             pltpu.VMEM((3, 4, 16, 128), BF16),
             pltpu.VMEM((2, 576, 128), F32),
@@ -476,8 +479,8 @@
             dma((3,)),
             dma((3,)),
             dma((3, 16)),
-            dma((3,)),
-            dma((3,)),
+            dma((1,)),
+            dma((1,)),
             dma((6,)),
             dma((6,)),
         ],

time: 98.7 us -> 97.6 us (0.989)
  Pallas kernels: 96.5 us -> 94.9 us
    pallas_call x1, Pallas kernels: 96.5 us -> 94.9 us  [shards(): pl.pallas_call(kernel, in_specs=[smem, hbm, hbm], out_specs=pl.BlockSpec(...]
where the time goes in v4:
time: 97.6 us; the launch traced here: 96.7 us
  Pallas kernels  94.9 us (97%)
  local copies, waits for them, and re-layouts  1.15 us (1%)
    pallas_call x1, Pallas kernels, shards(): pl.pallas_call(kernel, in_specs=[smem, hbm, hbm], out_specs=pl.BlockSpec(...  94.9 us

profile of v4, /device:TPU:1, one launch (start us, length us, event | category | flops | bytes accessed | tf_op | source)
XLA Modules:
  0.0 96.7 jit_solution(11887377979141958216)
XLA Ops:
  0.0 0.7 pad_add_fusion.small_ref
  0.7 94.9 %induction.1 = f32[768,512]{1,0:T(8,128)S(1)} custom-call(f32[1280]{0:T(1024)S(1)} %pad_add_fusion.small_ref, bf16[1536,512]{1,0:T(8,128)(2,1)} %bitcast.3, bf16[8,512,768]{2,1,0:T(8,128)(2,1)} %leg_hbm.1), custom_call_target="tpu_custom_call" | custom-call | tf_op jit(solution)/shard_map/induction/pallas_call | solution.py:447
  95.6 1.1 %copy.6 = f32[3,16,2,8,512]{4,3,2,1,0:T(8,128)} copy(f32[3,16,2,8,512]{4,3,2,1,0:T(8,128)S(1)} %bitcast.2) | data formatting | bytes 3145728

commit v5 on v4

--- a/solution.py
+++ b/solution.py
@@ -61,7 +61,12 @@
 
     fetch = pltpu.make_async_copy(fields_hbm, fbuf, in_sem.at[8])
     fetch.start()
-    fetches = [pltpu.make_async_copy(leg_hbm.at[s], leg.at[s], in_sem.at[s]) for s in range(8)]
+    fetches = []
+    for t in (0, 3, 1, 4, 2, 5):
+        lanes = pl.ds(t * 128, 128)
+        fetches.append(
+            pltpu.make_async_copy(leg_hbm.at[:, :, lanes], leg.at[:, :, lanes], in_sem.at[t])
+        )
     for f in fetches:
         f.start()
 
@@ -119,9 +124,9 @@
                 pltpu.make_async_copy(send1.at[q, dest], recv1.at[q, me], lsem1.at[q]).start()
 
     for q in range(3):
+        fetches[2 * q].wait()
+        fetches[2 * q + 1].wait()
         for s in range(8):
-            if q == 0:
-                fetches[s].wait()
             table = jnp.concatenate(
                 [leg[s, :, q * 128 : q * 128 + 128], leg[s, :, q * 128 + 384 : q * 128 + 512]],
                 axis=1,

time: 97.6 us -> 96.7 us (level)
  no operation moved by 1% of the time
where the time goes in v5:
time: 96.7 us; the launch traced here: 95.8 us
  Pallas kernels  94 us (97%)
  local copies, waits for them, and re-layouts  1.15 us (1%)
    pallas_call x1, Pallas kernels, shards(): pl.pallas_call(kernel, in_specs=[smem, hbm, hbm], out_specs=pl.BlockSpec(...  94 us

profile of v5, /device:TPU:1, one launch (start us, length us, event | category | flops | bytes accessed | tf_op | source)
XLA Modules:
  0.0 95.8 jit_solution(16267661413612569124)
XLA Ops:
  0.0 0.7 pad_add_fusion.small_ref
  0.7 94.0 %induction.1 = f32[768,512]{1,0:T(8,128)S(1)} custom-call(f32[1280]{0:T(1024)S(1)} %pad_add_fusion.small_ref, bf16[1536,512]{1,0:T(8,128)(2,1)} %bitcast.3, bf16[8,512,768]{2,1,0:T(8,128)(2,1)} %leg_hbm.1), custom_call_target="tpu_custom_call" | custom-call | tf_op jit(solution)/shard_map/induction/pallas_call | solution.py:452
  94.7 1.1 %copy.6 = f32[3,16,2,8,512]{4,3,2,1,0:T(8,128)} copy(f32[3,16,2,8,512]{4,3,2,1,0:T(8,128)S(1)} %bitcast.2) | data formatting | bytes 3145728
